TPU v7x, 128 devices: a whole 4x4x4 slice. The times are simulated.
128 devices in a mesh: site: 4 (over z), blk: 16 (over x, y), charge: 2 (over core).
Axes of the slice: x: 4, y: 4, z: 4, core: 2. Of those that a mesh axis runs over, the one named last changes fastest.
Arguments:
- theta: bfloat16 [4, 64, 128, 2048], P('site', ('blk', 'charge')), may hold values from -6 to 6
- boundary_env: bfloat16 [64, 18, 128, 128], P(('blk', 'charge')), may hold values from -1 to 1
- right_env: bfloat16 [4, 64, 18, 128, 128], P('site', ('blk', 'charge')), may hold values from -1 to 1
- site_tensors: bfloat16 [4, 2, 64, 4, 128, 128], P('site', None, ('blk', 'charge')), may hold values from -0.375 to 0.375
- site_mpo: bfloat16 [4, 2, 18, 18, 4, 4], P('site'), may hold values from -0.75 to 0.75
- bond_ops: bfloat16 [4, 18, 16, 16], P('site'), may hold values from -1 to 1
- block_energy: float32 [4, 64], P('site', ('blk', 'charge')), may hold values from 1 to 4
- sector_charge: int32 [4, 64], P('site', ('blk', 'charge')), may hold values from 0 to 63, as said below
- block_len: int32 [4, 64], P('site', ('blk', 'charge')), may hold values from 64 to 128
- channel_charge: int32 [18], replicated, may hold values from -1 to 1
Outputs:
- env_out: bfloat16 [4, 64, 18, 128, 128], P('site', ('blk', 'charge'))
- lanczos: bfloat16 [4, 64, 128, 2048], P('site', ('blk', 'charge'))
- coefficients: float32 [4, 2], P('site')
Inputs may be any that keep to these rules, and one draw needn't show every extreme that they name: `sector_charge`: in each section every label of 0 to 63 appears exactly once; the blocks held at index c of the charge axis carry labels of parity c.
All inputs are finite; a program needn't handle non-finite values.
Results may differ from a plain program's by a relative error of at most 0.03.
Values may be sent and summed in bfloat16 or wider, within the bound.
A program may use at most 128 MiB of HBM per device.

v0:
```python
import jax
import jax.numpy as jnp
from jax import lax
from jax.sharding import PartitionSpec as P

BS = 128
M = 2048
NS = 64


def from_behind(block, axis, distance):
    devices = range(lax.axis_size(axis))
    route = [(i - distance, i) for i in devices if i - distance in devices]
    return lax.ppermute(block, axis, route)


def from_partner(shard, axis, bit):
    return lax.ppermute(shard, axis, [(i, i ^ 1 << bit) for i in range(lax.axis_size(axis))])


def env_update(environ, tensors, site_op):

    def one_block(entries):
        env_block, site_blocks = entries
        left_part = jnp.einsum(
            "wab,sbc->wsac", env_block, site_blocks, preferred_element_type=jnp.float32
        ).astype(jnp.bfloat16)
        mixed = jnp.einsum(
            "wvts,wsac->vtac", site_op, left_part, preferred_element_type=jnp.float32
        ).astype(jnp.bfloat16)
        return jnp.einsum(
            "tab,vtac->vbc", site_blocks, mixed, preferred_element_type=jnp.float32
        ).astype(jnp.bfloat16)

    return lax.map(one_block, (environ, tensors))


def block_product(env_block, right_blocks, chosen, ops, charges):

    def segment(total_sum, entries):
        left_block, right_block, bond_op, charge = entries
        source_tile = lax.dynamic_index_in_dim(chosen, charge + 1, 0, keepdims=False)
        contracted = jnp.dot(left_block, source_tile, preferred_element_type=jnp.float32).astype(
            jnp.bfloat16
        )
        shaped = contracted.reshape(contracted.shape[0], ops.shape[1], -1)
        applied = jnp.einsum(
            "asb,bc->asc", shaped, right_block, preferred_element_type=jnp.float32
        ).astype(jnp.bfloat16)
        final = jnp.einsum("asc,st->atc", applied, bond_op, preferred_element_type=jnp.float32)
        return (total_sum + final.reshape(total_sum.shape), None)

    start_sum = jnp.zeros((chosen.shape[1], chosen.shape[2]), jnp.float32)
    return lax.scan(segment, start_sum, (env_block, right_blocks, ops, charges))[0]


def keep_same(values):
    return values


def pair_with(environ, tensors, site_ops):
    first = env_update(environ, tensors[0], site_ops[0])
    return env_update(first, tensors[1], site_ops[1])


def picker(wanted_labels, pieces):
    sign_pair = jnp.array([-1, 1], jnp.int32)
    wanted = wanted_labels[:, None] + sign_pair[None, :]
    incoming_tiles, incoming_tags = pieces
    matches = (incoming_tags[None, None, :] == wanted[:, :, None]).astype(jnp.bfloat16)
    picked = jnp.einsum(
        "kst,tam->ksam", matches, incoming_tiles, preferred_element_type=jnp.float32
    )
    return picked.astype(jnp.bfloat16)


def on_device(
    theta,
    boundary_env,
    right_env,
    site_tensors,
    site_mpo,
    bond_ops,
    block_energy,
    sector_charge,
    block_len,
    channel_charge,
):
    section = lax.axis_index("site")
    site_count = lax.axis_size("site")
    tensors = site_tensors[0]
    site_ops = site_mpo[0]

    def update_pair(environ):
        return pair_with(environ, tensors, site_ops)

    state = boundary_env
    env_in = boundary_env
    for segment in range(site_count):
        state = lax.cond(section == segment, update_pair, keep_same, state)
        if segment + 1 < site_count:
            received = from_behind(state, "site", 1)
            is_next = section == segment + 1
            state = jnp.where(is_next, received, state)
            env_in = jnp.where(is_next, received, env_in)
    labels = sector_charge[0]
    live_rows = block_len[0]
    row_mask = jnp.arange(theta.shape[2], dtype=jnp.int32)[None, :] < live_rows[:, None]
    theta_m = theta[0] * row_mask[:, :, None].astype(jnp.bfloat16)
    other_labels = from_partner(labels, "charge", 0)
    for_other = picker(
        other_labels,
        (
            lax.all_gather(theta_m, "blk", axis=0, tiled=True),
            lax.all_gather(labels, "blk", axis=0, tiled=True),
        ),
    )
    partner = from_partner(for_other, "charge", 0)
    chosen_all = jnp.stack([partner[:, 0], theta_m, partner[:, 1]], axis=1)
    ops = bond_ops[0]

    def per_block(entries):
        return block_product(entries[0], entries[1], entries[2], ops, channel_charge)

    product = lax.map(per_block, (env_in, right_env[0], chosen_all))
    theta_f = theta_m.astype(jnp.float32)
    product = (
        product * row_mask[:, :, None].astype(jnp.float32)
        - block_energy[0][:, None, None] * theta_f
    )
    entries_count = NS * BS * M
    correlation, norm_theta = lax.psum(
        (jnp.sum(theta_f * product), jnp.sum(theta_f * theta_f)), ("blk", "charge")
    )
    rayleigh = correlation / norm_theta
    residual = product - rayleigh * theta_f
    residual_sq = lax.psum(jnp.sum(residual * residual), ("blk", "charge"))
    mean_sq = residual_sq / entries_count
    lanczos = (residual / jnp.sqrt(mean_sq + 1e-06)).astype(jnp.bfloat16)
    coefficients = jnp.stack([rayleigh, jnp.sqrt(mean_sq)])[None, :]
    return (state[None], lanczos[None], coefficients)


def solution(mesh):
    return jax.shard_map(
        on_device,
        mesh=mesh,
        in_specs=(
            P("site", ("blk", "charge"), None, None),
            P(("blk", "charge"), None, None, None),
            P("site", ("blk", "charge"), None, None, None),
            P("site", None, ("blk", "charge"), None, None, None),
            P("site", None, None, None, None, None),
            P("site", None, None, None),
            P("site", ("blk", "charge")),
            P("site", ("blk", "charge")),
            P("site", ("blk", "charge")),
            P(),
        ),
        out_specs=(
            P("site", ("blk", "charge"), None, None, None),
            P("site", ("blk", "charge"), None, None),
            P("site", None),
        ),
        check_vma=False,
    )
```

profile of v0, /device:TPU:97, one launch (start us, length us, event | category | flops | bytes accessed | tf_op | source)
XLA Modules:
  0.0 685.1 jit_solution(11959686821084895500)
XLA Ops:
  9.1 2.4 bitcast_multiply_fusion
  18.5 13.5 %all-reduce = s32[32]{0:T(128)S(1)} all-reduce(s32[32]{0:T(128)S(1)} %bitcast_dynamic-update-slice_fusion.1), channel_id=2, replica_groups=mesh['site'=4,'blk'=16,'charge'=2] {'blk'}, use_global_device_ids=true, to_apply=%add | all-reduce | flops 32 | bytes 256
  32.1 11.6 %collective-permute-done = bf16[2,18,128,128]{3,2,1,0:T(8,128)(2,1)S(1)} collective-permute-done((bf16[2,18,128,128]{3,2,1,0:T(8,128)(2,1)}, bf16[2,18,128,128]{3,2,1,0:T(8,128)(2,1)S(1)}, u32[]{:S(2)}, u32[]{:S(2)}) %collective-permute-start) | collective-permute-done | bytes 1179680 | tf_op jit(solution)/shard_map/ppermute | solution.py:14
  43.7 1.8 broadcast_select_fusion
  45.6 1.5 collective-permute-start.1
  47.0 77.2 %all-gather.3.cloned.1.call-done = bf16[32,128,2048]{2,1,0:T(8,128)(2,1)} async-done(((bf16[2,128,2048]{2,1,0:T(8,128)(2,1)}), bf16[32,128,2048]{2,1,0:T(8,128)(2,1)}) %all-gather.3.cloned.1.call-update) | async-done | bytes 16777232 | tf_op jit(solution)/shard_map/all_gather | solution.py:114
  124.2 26.1 %fusion.233 = bf16[2,2,128,2048]{3,1,2,0:T(2,128)(2,1)} fusion(bf16[32,128,2048]{2,1,0:T(8,128)(2,1)} %all-gather.3.cloned.1.call-done, s32[32]{0:T(128)S(1)} %all-reduce, s32[2,2]{1,0:T(2,128)S(1)} %broadcast_add_fusion), kind=kOutput, calls=%fused_computation.203 | convolution fusion | flops 68157568 | bytes 18874512 | tf_op jit(solution)/shard_map/kst,tam->ksam/dot_general | solution.py:71
  151.6 9.2 %collective-permute-start.2 = (bf16[2,18,128,128]{3,2,1,0:T(8,128)(2,1)S(1)}, bf16[2,18,128,128]{3,2,1,0:T(8,128)(2,1)}, u32[]{:S(2)}, u32[]{:S(2)}) collective-permute-start(bf16[2,18,128,128]{3,2,1,0:T(8,128)(2,1)S(1)} %get-tuple-element.589), channel_id=1, source_target_pairs={{0,32},{32,64},{64,96},{1,33},{33,65},{65,97},{2,34},{34,66},{66,9... | collective-permute-start | bytes 3538952 | tf_op jit(solution)/shard_map/ppermute | solution.py:14
  160.8 1.7 copy.99
  162.5 2.2 copy_multiply_fusion
  164.7 85.6 %collective-permute-done.2 = bf16[2,18,128,128]{3,2,1,0:T(8,128)(2,1)} collective-permute-done((bf16[2,18,128,128]{3,2,1,0:T(8,128)(2,1)S(1)}, bf16[2,18,128,128]{3,2,1,0:T(8,128)(2,1)}, u32[]{:S(2)}, u32[]{:S(2)}) %collective-permute-start.2) | collective-permute-done | bytes 1179680 | tf_op jit(solution)/shard_map/ppermute | solution.py:14
  250.4 2.7 select_select_fusion
  253.1 5.6 fusion.247
  258.6 7.1 %pad_maximum_fusion = bf16[2,3,128,2048]{3,1,2,0:T(4,128)(2,1)S(1)} fusion(bf16[2,1,128,2048]{3,1,2,0:T(2,128)(2,1)S(1)} %get-tuple-element.724, bf16[2,1,128,2048]{3,1,2,0:T(2,128)(2,1)S(1)} %copy_multiply_fusion, bf16[2,1,128,2048]{3,1,2,0:T(2,128)(2,1)S(1)} %get-tuple-element.723), kind=kLoop, calls=%fused_computation.198 | loop fusion | flops 9437184 | bytes 6291456 | tf_op jit(solution)/shard_map/stack | solution.py:119
  265.8 3.9 copy.100
  269.7 211.9 %while.113 = (s32[]{:T(128)}, f32[2,128,2048]{2,1,0:T(8,128)}, bf16[2,18,128,128]{3,2,1,0:T(8,128)(2,1)S(1)}, bf16[2,18,128,128]{3,2,1,0:T(8,128)(2,1)}, bf16[2,...) while((s32[]{:T(128)}, f32[2,128,2048]{2,1,0:T(8,128)}, ...), condition=%wide.region_27.28_spmd, body=%wide.region_24.27_spmd.sunk | while | flops 143654912 | bytes 23926256 | solution.py:125
  269.7 2.4 dynamic-slice_bitcast_fusion.5
  272.1 2.7 dynamic-slice_bitcast_fusion.6
  274.8 99.1 %while.114 = (s32[]{:T(128)}, f32[128,2048]{1,0:T(8,128)S(1)}, bf16[18,16,16]{1,2,0:T(8,128)(2,1)}, bf16[18,128,128]{2,1,0:T(8,128)(2,1)}, s32[18]{0:T(128)S(1)}...) while((s32[]{:T(128)}, f32[128,2048]{1,0:T(8,128)S(1)}, ...), condition=%wide.region_26.26_spmd.clone, body=%wide.region_25.25_spmd.clone.sunk | while | flops 143654912 | bytes 6886593 | solution.py:54
  375.6 2.4 dynamic-slice_bitcast_fusion.5
  378.0 2.7 dynamic-slice_bitcast_fusion.6
  380.7 99.1 %while.114 = (s32[]{:T(128)}, f32[128,2048]{1,0:T(8,128)S(1)}, bf16[18,16,16]{1,2,0:T(8,128)(2,1)}, bf16[18,128,128]{2,1,0:T(8,128)(2,1)}, s32[18]{0:T(128)S(1)}...) while((s32[]{:T(128)}, f32[128,2048]{1,0:T(8,128)S(1)}, ...), condition=%wide.region_26.26_spmd.clone, body=%wide.region_25.25_spmd.clone.sunk | while | flops 143654912 | bytes 6886593 | solution.py:54
  382.8 1.4 fusion.325
  399.3 1.4 fusion.325
  415.8 1.4 fusion.325
  481.5 3.8 fusion.238
  485.3 68.7 %all-reduce.1 = (f32[]{:T(128)}, f32[]{:T(128)}) all-reduce(f32[]{:T(128)} %get-tuple-element.594, f32[]{:T(128)} %get-tuple-element.593), channel_id=1, replica_groups=mesh['site'=4,'blk'=16,'charge'=2] {'blk','charge'}, use_global_device_ids=true, to_apply=%region_29.30 | all-reduce | flops 2 | bytes 16 | tf_op jit(solution)/shard_map/psum | solution.py:132
  555.4 3.3 multiply_reduce_fusion
  558.7 48.6 %conditional.7 = (bf16[1,2,18,128,128]{4,3,2,1,0:T(8,128)(2,1)}) conditional(s32[]{:T(128)} %convert_element_type.194, (bf16[2,18,128,128]{3,2,1,0:T(8,128)(2,1)S(1)}) %tuple.289, (bf16[2,2,4,128,128]{3,4,2,1,0:T(8,128)(2,1)}, bf16[2,18,18,4,4]{1,2,4,3,0:T(8,128)(2,1)}, bf16[2,18,128,128]{3,2,1,0:T(8,128)(2,1)S(1)}) %tuple.290), branch_computations={%region_18.19_spmd, %region_19.24_spmd} | conditional | flops 1553006592 | bytes 31303274 | solution.py:100
  558.7 1.9 slice_bitcast_fusion.12
  560.6 1.6 slice_bitcast_fusion.14
  562.5 21.7 %while.109 = (s32[]{:T(128)}, bf16[2,18,128,128]{2,3,1,0:T(8,128)(2,1)S(1)}, bf16[2,4,128,128]{2,3,1,0:T(8,128)(2,1)}, bf16[2,18,128,128]{3,2,1,0:T(8,128)(2,1)S(1)}, bf16[18,18,4,4]{0,1,3,2:T(8,128)(2,1)}, /*index=5*/s32[]{:T(128)}) while((s32[]{:T(128)}, bf16[2,18,128,128]{2,3,1,0:T(8,128)(2,1)S(1)}, bf16[2,4,128,128]{2,3,1,0:T(8,128)(2,1)}, ...), condition=%wide.region_21.21_spmd, body=%wide.region_20.20_spmd.sunk | while | flops 776503296 | bytes 12768005 | solution.py:35
  562.7 1.7 convert_bitcast_fusion.16
  564.4 7.2 %fusion.333 = bf16[18,4,128,128]{2,0,1,3:T(8,128)(2,1)S(1)} fusion(bf16[18,4,128,128,1]{2,3,0,1,4:T(8,128)(2,1)S(1)} %convert_bitcast_fusion.16, bf16[18,18,4,4]{0,1,3,2:T(8,128)(2,1)S(1)} %copy-done.20), kind=kOutput, calls=%fused_computation.133.clone.1 | convolution fusion | flops 171048960 | bytes 4728960 | tf_op jit(solution)/shard_map/cond/branch_1_fun/while/body/eval_jaxpr/wvts,wsac->vtac/dot_general | solution.py:28
  571.6 1.7 fusion.334
  573.4 1.7 convert_bitcast_fusion.16
  575.2 7.2 %fusion.333 = bf16[18,4,128,128]{2,0,1,3:T(8,128)(2,1)S(1)} fusion(bf16[18,4,128,128,1]{2,3,0,1,4:T(8,128)(2,1)S(1)} %convert_bitcast_fusion.16, bf16[18,18,4,4]{0,1,3,2:T(8,128)(2,1)S(1)} %copy-done.20), kind=kOutput, calls=%fused_computation.133.clone.1 | convolution fusion | flops 171048960 | bytes 4728960 | tf_op jit(solution)/shard_map/cond/branch_1_fun/while/body/eval_jaxpr/wvts,wsac->vtac/dot_general | solution.py:28
  582.4 1.7 fusion.334
  584.4 21.3 %while.110 = (s32[]{:T(128)}, bf16[2,18,128,128]{2,3,1,0:T(8,128)(2,1)S(1)}, bf16[2,4,128,128]{2,3,1,0:T(8,128)(2,1)}, bf16[2,18,128,128]{2,3,1,0:T(8,128)(2,1)S...) while((s32[]{:T(128)}, bf16[2,18,128,128]{2,3,1,0:T(8,128)(2,1)S(1)}, ...), condition=%wide.region_23.23_spmd, body=%wide.region_22.22_spmd.sunk | while | flops 776503296 | bytes 12726505 | solution.py:35
  584.4 1.7 convert_bitcast_fusion.17
  586.1 7.2 %fusion.341 = bf16[18,4,128,128]{2,0,1,3:T(8,128)(2,1)S(1)} fusion(bf16[18,4,128,128,1]{2,3,0,1,4:T(8,128)(2,1)S(1)} %convert_bitcast_fusion.17, bf16[18,18,4,4]{0,1,3,2:T(8,128)(2,1)S(1)} %get-tuple-element.1151), kind=kOutput, calls=%fused_computation.153.clone.1 | convolution fusion | flops 171048960 | bytes 4728960 | tf_op jit(solution)/shard_map/cond/branch_1_fun/while/body/eval_jaxpr/wvts,wsac->vtac/dot_general | solution.py:28
  593.3 1.7 fusion.342
  595.1 1.7 convert_bitcast_fusion.17
  596.8 7.2 %fusion.341 = bf16[18,4,128,128]{2,0,1,3:T(8,128)(2,1)S(1)} fusion(bf16[18,4,128,128,1]{2,3,0,1,4:T(8,128)(2,1)S(1)} %convert_bitcast_fusion.17, bf16[18,18,4,4]{0,1,3,2:T(8,128)(2,1)S(1)} %get-tuple-element.1151), kind=kOutput, calls=%fused_computation.153.clone.1 | convolution fusion | flops 171048960 | bytes 4728960 | tf_op jit(solution)/shard_map/cond/branch_1_fun/while/body/eval_jaxpr/wvts,wsac->vtac/dot_general | solution.py:28
  604.0 1.7 fusion.342
  605.7 1.4 copy.177
  607.4 65.9 %psum.23 = f32[]{:T(128)} all-reduce(f32[]{:T(128)} %multiply_reduce_fusion), channel_id=1, replica_groups=mesh['site'=4,'blk'=16,'charge'=2] {'blk','charge'}, use_global_device_ids=true, to_apply=%region_33.34 | all-reduce | flops 1 | bytes 8 | tf_op jit(solution)/shard_map/psum | solution.py:137
  674.0 3.3 fusion.240
  (257 shorter events, 158.0 us)
Async XLA Ops:
  7.2 4.4 copy-start.18
  7.2 5.4 copy-start.17
  7.2 117.0 %all-gather.3.cloned.1.call-start = ((), (), s32[]{:S(2)}) async-start(), calls=%async_computation | async-start | bytes 17825792 | tf_op jit(solution)/shard_map/all_gather | solution.py:114
  8.6 0.5 copy-start.21
  9.1 4.5 copy-start.2
  13.6 2.3 copy-start.26
  13.6 3.4 copy-start.28
  13.6 18.4 %copy-start.25 = (s32[2]{0:T(128)S(1)}, s32[2]{0:T(128)}, u32[]{:S(2)}) copy-start(s32[2]{0:T(128)} %constant.168.clone) | copy-start | bytes 28
  14.7 29.0 %collective-permute-start = (bf16[2,18,128,128]{3,2,1,0:T(8,128)(2,1)}, bf16[2,18,128,128]{3,2,1,0:T(8,128)(2,1)S(1)}, u32[]{:S(2)}, u32[]{:S(2)}) collective-permute-start(bf16[2,18,128,128]{3,2,1,0:T(8,128)(2,1)} %get-tuple-element.585), channel_id=1, source_target_pairs={{0,32},{32,64},{64,96},{1,33},{33,65},{65,97},{2,34},{34,66},{66,9... | collective-permute-start | bytes 3538952 | tf_op jit(solution)/shard_map/ppermute | solution.py:14
  16.0 16.0 %collective-permute-start.3 = (s32[2]{0:T(128)S(1)}, s32[2]{0:T(128)S(1)}, u32[]{:S(2)}, u32[]{:S(2)}) collective-permute-start(s32[2]{0:T(128)S(1)} %bitcast.620), channel_id=1, source_target_pairs={{0,1},{1,0},{2,3},{3,2},{4,5},{5,4},{6,7},{7,6},{8,9},{9,8},{10,11... | collective-permute-start | bytes 32 | tf_op jit(solution)/shard_map/ppermute | solution.py:18
  43.7 1.8 copy-start.8
  45.6 105.5 %collective-permute-start.1 = (bf16[2,18,128,128]{3,2,1,0:T(8,128)(2,1)S(1)}, bf16[2,18,128,128]{3,2,1,0:T(8,128)(2,1)}, u32[]{:S(2)}, u32[]{:S(2)}) collective-permute-start(bf16[2,18,128,128]{3,2,1,0:T(8,128)(2,1)S(1)} %get-tuple-element.587), channel_id=1, source_target_pairs={{0,32},{32,64},{64,96},{1,33},{33,65},{65,97},{2,34},{34,66},{66,9... | collective-permute-start | bytes 3538952 | tf_op jit(solution)/shard_map/ppermute | solution.py:14
  150.3 102.7 %collective-permute-start.4 = (bf16[2,2,128,2048]{3,1,2,0:T(2,128)(2,1)}, bf16[2,2,128,2048]{3,1,2,0:T(2,128)(2,1)}, u32[]{:S(2)}, u32[]{:S(2)}) collective-permute-start(bf16[2,2,128,2048]{3,1,2,0:T(2,128)(2,1)} %fusion.233), channel_id=1, source_target_pairs={{0,1},{1,0},{2,3},{3,2},{4,5},{5,4},{6,7},{7,6},{8,9},{9,8},{10,11... | collective-permute-start | bytes 6291464 | tf_op jit(solution)/shard_map/ppermute | solution.py:18
  151.2 11.3 %copy-start = (bf16[1,2,128,2048]{3,2,1,0:T(8,128)(2,1)S(1)}, bf16[1,2,128,2048]{3,2,1,0:T(8,128)(2,1)}, u32[]{:S(2)}) copy-start(bf16[1,2,128,2048]{3,2,1,0:T(8,128)(2,1)} %param.39) | copy-start | bytes 3145732
  151.2 11.3 %copy-start.22 = (bf16[2,128]{1,0:T(2,128)(2,1)S(1)}, bf16[2,128]{1,0:T(2,128)(2,1)}, u32[]{:S(2)}) copy-start(bf16[2,128]{1,0:T(2,128)(2,1)} %copy-done.21) | copy-start | bytes 1540
  151.6 98.7 %collective-permute-start.2 = (bf16[2,18,128,128]{3,2,1,0:T(8,128)(2,1)S(1)}, bf16[2,18,128,128]{3,2,1,0:T(8,128)(2,1)}, u32[]{:S(2)}, u32[]{:S(2)}) collective-permute-start(bf16[2,18,128,128]{3,2,1,0:T(8,128)(2,1)S(1)} %get-tuple-element.589), channel_id=1, source_target_pairs={{0,32},{32,64},{64,96},{1,33},{33,65},{65,97},{2,34},{34,66},{66,9... | collective-permute-start | bytes 3538952 | tf_op jit(solution)/shard_map/ppermute | solution.py:14
  162.5 87.9 %copy-start.9 = (bf16[2,18,128,128]{3,2,1,0:T(8,128)(2,1)S(1)}, bf16[2,18,128,128]{3,2,1,0:T(8,128)(2,1)}, u32[]{:S(2)}) copy-start(bf16[2,18,128,128]{3,2,1,0:T(8,128)(2,1)} %copy-done.8) | copy-start | bytes 3538948
  265.8 3.9 copy-start.27
  269.7 211.9 %copy-start.23 = (f32[2,128]{1,0:T(2,128)S(1)}, f32[2,128]{1,0:T(2,128)}, u32[]{:S(2)}) copy-start(f32[2,128]{1,0:T(2,128)} %get-tuple-element.727) | copy-start | bytes 3076
  269.7 211.9 %copy-start.24 = (f32[1,2]{1,0:T(1,128)S(1)}, f32[1,2]{1,0:T(1,128)}, u32[]{:S(2)}) copy-start(f32[1,2]{1,0:T(1,128)} %param.45) | copy-start | bytes 28
  269.7 5.2 copy-start.4
  374.0 1.6 copy-start.5
  375.6 5.1 copy-start.4
  479.9 1.6 copy-start.5
  481.5 73.8 %copy-start.1 = (bf16[1,2,128,2048]{3,2,1,0:T(8,128)(2,1)S(1)}, bf16[1,2,128,2048]{3,2,1,0:T(8,128)(2,1)}, u32[]{:S(2)}) copy-start(bf16[1,2,128,2048]{3,2,1,0:T(8,128)(2,1)} %param.39) | copy-start | bytes 3145732
  481.5 73.8 %copy-start.3 = (bf16[2,18,128,128]{3,2,1,0:T(8,128)(2,1)S(1)}, bf16[2,18,128,128]{3,2,1,0:T(8,128)(2,1)}, u32[]{:S(2)}) copy-start(bf16[2,18,128,128]{3,2,1,0:T(8,128)(2,1)} %get-tuple-element.726) | copy-start | bytes 3538948
  562.7 1.7 copy-start.20
  564.4 7.2 %copy-start.14 = (bf16[2,4,128,128]{2,3,1,0:T(8,128)(2,1)S(1)}, bf16[2,4,128,128]{2,3,1,0:T(8,128)(2,1)}, u32[]{:S(2)}) copy-start(bf16[2,4,128,128]{2,3,1,0:T(8,128)(2,1)} %get-tuple-element.1131) | copy-start | bytes 786436 | tf_op jit(solution)/shard_map/cond/branch_1_fun/while
  573.4 1.7 copy-start.20
  575.2 7.2 %copy-start.14 = (bf16[2,4,128,128]{2,3,1,0:T(8,128)(2,1)S(1)}, bf16[2,4,128,128]{2,3,1,0:T(8,128)(2,1)}, u32[]{:S(2)}) copy-start(bf16[2,4,128,128]{2,3,1,0:T(8,128)(2,1)} %get-tuple-element.1131) | copy-start | bytes 786436 | tf_op jit(solution)/shard_map/cond/branch_1_fun/while
  586.1 7.2 %copy-start.11 = (bf16[2,4,128,128]{2,3,1,0:T(8,128)(2,1)S(1)}, bf16[2,4,128,128]{2,3,1,0:T(8,128)(2,1)}, u32[]{:S(2)}) copy-start(bf16[2,4,128,128]{2,3,1,0:T(8,128)(2,1)} %get-tuple-element.1149) | copy-start | bytes 786436 | tf_op jit(solution)/shard_map/cond/branch_1_fun/while
  596.7 7.2 %copy-start.11 = (bf16[2,4,128,128]{2,3,1,0:T(8,128)(2,1)S(1)}, bf16[2,4,128,128]{2,3,1,0:T(8,128)(2,1)}, u32[]{:S(2)}) copy-start(bf16[2,4,128,128]{2,3,1,0:T(8,128)(2,1)} %get-tuple-element.1149) | copy-start | bytes 786436 | tf_op jit(solution)/shard_map/cond/branch_1_fun/while
Sparse Core Ops, SparseCore 0:
  11.7 112.4 all-gather.2
where the time goes:
time: 698 us; the launch traced here: 685 us
  waiting for transfers between devices  174 us (25%)
  matrix products  161 us (23%)
  blocking collectives  148 us (21%)
  local copies, waits for them, and re-layouts  62.4 us (9%)
  other arithmetic  56 us (8%)
  loops' own time  52.4 us (8%)
  between operations  17.4 us (2%)
  starting transfers between devices  13.8 us (2%)
    ppermute x3, waiting for transfers between devices, from_behind(): return lax.ppermute(block, axis, route)  97.3 us
    all_gather x1, waiting for transfers between devices, on_device(): lax.all_gather(theta_m, 'blk', axis=0, tiled=True)  77.2 us
    psum x1, blocking collectives, on_device(): lax.psum((jnp.sum(theta_f * product), jnp.sum(theta_f * theta_f)), ('blk'...  68.7 us
    psum x1, blocking collectives, on_device(): residual_sq = lax.psum(jnp.sum(residual * residual), ('blk', 'charge'))  65.9 us
    another operation x2, loops' own time, block_product(): lax.scan(segment, start_sum, (env_block, right_blocks, ops, charges))[0]  51.2 us
    dot_general x36, matrix products, segment(): jnp.dot(left_block, source_tile, preferred_element_type=jnp.float32)  48.7 us
    dot_general x36, matrix products, segment(): jnp.einsum('asc,st->atc', applied, bond_op, preferred_element_type=jnp.fl...  43.4 us
    dot_general x4, matrix products, one_block(): jnp.einsum('wvts,wsac->vtac', site_op, left_part, preferred_element_type=...  28.8 us
  transfers between devices with their start and end apart: 6, of which 3 were waited for; matrix products, arithmetic and copies ran while one was open for 6% of the time, Pallas kernels for 0%

commit v1 on v0

--- a/solution.py
+++ b/solution.py
@@ -1,3 +1,4 @@
+import functools
 import jax
 import jax.numpy as jnp
 from jax import lax
@@ -6,6 +7,15 @@
 BS = 128
 M = 2048
 NS = 64
+
+
+def fix_ladders(my_data, shard_axis, axis_tag):
+    for i0 in (shard_axis, axis_tag):
+        my_data = jax.lax.psum(my_data, i0)
+    return my_data
+
+
+raise_the_sources_all = functools.partial(fix_ladders, shard_axis="blk", axis_tag="charge")
 
 
 def from_behind(block, axis, distance):
@@ -129,8 +139,8 @@
         - block_energy[0][:, None, None] * theta_f
     )
     entries_count = NS * BS * M
-    correlation, norm_theta = lax.psum(
-        (jnp.sum(theta_f * product), jnp.sum(theta_f * theta_f)), ("blk", "charge")
+    correlation, norm_theta = raise_the_sources_all(
+        (jnp.sum(theta_f * product), jnp.sum(theta_f * theta_f))
     )
     rayleigh = correlation / norm_theta
     residual = product - rayleigh * theta_f

time: 698 us -> 664 us (0.951)
  blocking collectives: 148 us -> 126 us
  loops' own time: 52.4 us -> 43.2 us
    psum x1 -> x2, blocking collectives: 68.7 us -> 49.8 us  [fix_ladders(): my_data = jax.lax.psum(my_data, i0)]
    another operation x2, loops' own time: 51.2 us -> 42 us  [block_product(): lax.scan(segment, start_sum, (env_block, right_blocks, ops, charges))[0]]
where the time goes in v1:
time: 664 us; the launch traced here: 651 us
  waiting for transfers between devices  174 us (26%)
  matrix products  161 us (24%)
  blocking collectives  126 us (19%)
  local copies, waits for them, and re-layouts  59.4 us (9%)
  other arithmetic  55.9 us (8%)
  loops' own time  43.2 us (7%)
  between operations  17.5 us (3%)
  starting transfers between devices  13.8 us (2%)
    ppermute x3, waiting for transfers between devices, from_behind(): return lax.ppermute(block, axis, route)  97.2 us
    all_gather x1, waiting for transfers between devices, on_device(): lax.all_gather(theta_m, 'blk', axis=0, tiled=True)  77.2 us
    psum x1, blocking collectives, on_device(): residual_sq = lax.psum(jnp.sum(residual * residual), ('blk', 'charge'))  62.9 us
    psum x2, blocking collectives, fix_ladders(): my_data = jax.lax.psum(my_data, i0)  49.8 us
    dot_general x36, matrix products, segment(): jnp.dot(left_block, source_tile, preferred_element_type=jnp.float32)  48.7 us
    dot_general x36, matrix products, segment(): jnp.einsum('asc,st->atc', applied, bond_op, preferred_element_type=jnp.fl...  43.4 us
    another operation x2, loops' own time, block_product(): lax.scan(segment, start_sum, (env_block, right_blocks, ops, charges))[0]  42 us
    dot_general x4, matrix products, one_block(): jnp.einsum('wvts,wsac->vtac', site_op, left_part, preferred_element_type=...  28.8 us
  transfers between devices with their start and end apart: 6, of which 3 were waited for; matrix products, arithmetic and copies ran while one was open for 6% of the time, Pallas kernels for 0%

profile of v1, /device:TPU:97, one launch (start us, length us, event | category | flops | bytes accessed | tf_op | source)
XLA Modules:
  0.0 651.1 jit_solution(7070397695533457432)
XLA Ops:
  7.2 1.4 fusion.244
  9.1 2.4 bitcast_multiply_fusion
  18.5 13.5 %all-reduce = s32[32]{0:T(128)S(1)} all-reduce(s32[32]{0:T(128)S(1)} %bitcast_dynamic-update-slice_fusion.1), channel_id=2, replica_groups=mesh['site'=4,'blk'=16,'charge'=2] {'blk'}, use_global_device_ids=true, to_apply=%add | all-reduce | flops 32 | bytes 256
  32.1 11.6 %collective-permute-done = bf16[2,18,128,128]{3,2,1,0:T(8,128)(2,1)S(1)} collective-permute-done((bf16[2,18,128,128]{3,2,1,0:T(8,128)(2,1)}, bf16[2,18,128,128]{3,2,1,0:T(8,128)(2,1)S(1)}, u32[]{:S(2)}, u32[]{:S(2)}) %collective-permute-start) | collective-permute-done | bytes 1179680 | tf_op jit(solution)/shard_map/ppermute | solution.py:24
  43.7 1.8 broadcast_select_fusion
  45.6 1.5 collective-permute-start.1
  47.0 77.2 %all-gather.3.cloned.1.call-done = bf16[32,128,2048]{2,1,0:T(8,128)(2,1)} async-done(((bf16[2,128,2048]{2,1,0:T(8,128)(2,1)}), bf16[32,128,2048]{2,1,0:T(8,128)(2,1)}) %all-gather.3.cloned.1.call-update) | async-done | bytes 16777232 | tf_op jit(solution)/shard_map/all_gather | solution.py:124
  124.2 26.1 %fusion.233 = bf16[2,2,128,2048]{3,1,2,0:T(2,128)(2,1)} fusion(bf16[32,128,2048]{2,1,0:T(8,128)(2,1)} %all-gather.3.cloned.1.call-done, s32[32]{0:T(128)S(1)} %all-reduce, s32[2,2]{1,0:T(2,128)S(1)} %broadcast_add_fusion), kind=kOutput, calls=%fused_computation.203 | convolution fusion | flops 68157568 | bytes 18874512 | tf_op jit(solution)/shard_map/kst,tam->ksam/dot_general | solution.py:81
  151.6 9.2 %collective-permute-start.2 = (bf16[2,18,128,128]{3,2,1,0:T(8,128)(2,1)S(1)}, bf16[2,18,128,128]{3,2,1,0:T(8,128)(2,1)}, u32[]{:S(2)}, u32[]{:S(2)}) collective-permute-start(bf16[2,18,128,128]{3,2,1,0:T(8,128)(2,1)S(1)} %get-tuple-element.589), channel_id=1, source_target_pairs={{0,32},{32,64},{64,96},{1,33},{33,65},{65,97},{2,34},{34,66},{66,9... | collective-permute-start | bytes 3538952 | tf_op jit(solution)/shard_map/ppermute | solution.py:24
  160.9 1.7 copy.99
  162.5 2.2 copy_multiply_fusion
  164.8 85.6 %collective-permute-done.2 = bf16[2,18,128,128]{3,2,1,0:T(8,128)(2,1)} collective-permute-done((bf16[2,18,128,128]{3,2,1,0:T(8,128)(2,1)S(1)}, bf16[2,18,128,128]{3,2,1,0:T(8,128)(2,1)}, u32[]{:S(2)}, u32[]{:S(2)}) %collective-permute-start.2) | collective-permute-done | bytes 1179680 | tf_op jit(solution)/shard_map/ppermute | solution.py:24
  250.4 2.7 select_select_fusion
  253.1 5.6 fusion.247
  258.7 7.1 %pad_maximum_fusion = bf16[2,3,128,2048]{3,1,2,0:T(4,128)(2,1)S(1)} fusion(bf16[2,1,128,2048]{3,1,2,0:T(2,128)(2,1)S(1)} %get-tuple-element.726, bf16[2,1,128,2048]{3,1,2,0:T(2,128)(2,1)S(1)} %copy_multiply_fusion, bf16[2,1,128,2048]{3,1,2,0:T(2,128)(2,1)S(1)} %get-tuple-element.725), kind=kLoop, calls=%fused_computation.198 | loop fusion | flops 9437184 | bytes 6291456 | tf_op jit(solution)/shard_map/stack | solution.py:129
  265.8 3.9 copy.100
  269.7 199.8 %while.113 = (s32[]{:T(128)}, f32[2,128,2048]{2,1,0:T(8,128)}, bf16[2,18,128,128]{3,2,1,0:T(8,128)(2,1)S(1)}, bf16[2,18,128,128]{3,2,1,0:T(8,128)(2,1)}, bf16[2,...) while((s32[]{:T(128)}, f32[2,128,2048]{2,1,0:T(8,128)}, ...), condition=%wide.region_27.28_spmd, body=%wide.region_24.27_spmd.sunk | while | flops 143654912 | bytes 23926256 | solution.py:135
  269.7 2.4 dynamic-slice_bitcast_fusion.5
  272.1 2.8 dynamic-slice_bitcast_fusion.6
  274.9 93.1 %while.114 = (s32[]{:T(128)}, f32[128,2048]{1,0:T(8,128)S(1)}, bf16[18,16,16]{1,2,0:T(8,128)(2,1)}, bf16[18,128,128]{2,1,0:T(8,128)(2,1)}, s32[18]{0:T(128)S(1)}...) while((s32[]{:T(128)}, f32[128,2048]{1,0:T(8,128)S(1)}, ...), condition=%wide.region_26.26_spmd.clone, body=%wide.region_25.25_spmd.clone.sunk | while | flops 143654912 | bytes 6886593 | solution.py:64
  307.6 1.4 fusion.325
  369.6 2.4 dynamic-slice_bitcast_fusion.5
  372.0 2.8 dynamic-slice_bitcast_fusion.6
  374.8 93.1 %while.114 = (s32[]{:T(128)}, f32[128,2048]{1,0:T(8,128)S(1)}, bf16[18,16,16]{1,2,0:T(8,128)(2,1)}, bf16[18,128,128]{2,1,0:T(8,128)(2,1)}, s32[18]{0:T(128)S(1)}...) while((s32[]{:T(128)}, f32[128,2048]{1,0:T(8,128)S(1)}, ...), condition=%wide.region_26.26_spmd.clone, body=%wide.region_25.25_spmd.clone.sunk | while | flops 143654912 | bytes 6886593 | solution.py:64
  469.5 3.8 fusion.238
  473.3 37.4 %all-reduce.1 = (f32[]{:T(128)}, f32[]{:T(128)}) all-reduce(f32[]{:T(128)} %get-tuple-element.594, f32[]{:T(128)} %get-tuple-element.593), channel_id=1, replica_groups=mesh['site'=4,'blk'=16,'charge'=2] {'blk'}, use_global_device_ids=true, to_apply=%region_29.30 | all-reduce | flops 2 | bytes 16 | tf_op jit(solution)/shard_map/psum | solution.py:14
  510.7 12.4 %all-reduce.2 = (f32[]{:T(128)}, f32[]{:T(128)}) all-reduce(f32[]{:T(128)} %get-tuple-element.703, f32[]{:T(128)} %get-tuple-element.704), channel_id=1, replica_groups=mesh['site'=4,'blk'=16,'charge'=2] {'charge'}, use_global_device_ids=true, to_apply=%region_30.31 | all-reduce | flops 2 | bytes 16 | tf_op jit(solution)/shard_map/psum | solution.py:14
  524.5 3.2 multiply_reduce_fusion
  527.7 48.6 %conditional.7 = (bf16[1,2,18,128,128]{4,3,2,1,0:T(8,128)(2,1)}) conditional(s32[]{:T(128)} %convert_element_type.194, (bf16[2,18,128,128]{3,2,1,0:T(8,128)(2,1)S(1)}) %tuple.289, (bf16[2,2,4,128,128]{3,4,2,1,0:T(8,128)(2,1)}, bf16[2,18,18,4,4]{1,2,4,3,0:T(8,128)(2,1)}, bf16[2,18,128,128]{3,2,1,0:T(8,128)(2,1)S(1)}) %tuple.290), branch_computations={%region_18.19_spmd, %region_19.24_spmd} | conditional | flops 1553006592 | bytes 31303274 | solution.py:110
  527.7 1.9 slice_bitcast_fusion.12
  529.6 1.6 slice_bitcast_fusion.14
  531.5 21.7 %while.109 = (s32[]{:T(128)}, bf16[2,18,128,128]{2,3,1,0:T(8,128)(2,1)S(1)}, bf16[2,4,128,128]{2,3,1,0:T(8,128)(2,1)}, bf16[2,18,128,128]{3,2,1,0:T(8,128)(2,1)S(1)}, bf16[18,18,4,4]{0,1,3,2:T(8,128)(2,1)}, /*index=5*/s32[]{:T(128)}) while((s32[]{:T(128)}, bf16[2,18,128,128]{2,3,1,0:T(8,128)(2,1)S(1)}, bf16[2,4,128,128]{2,3,1,0:T(8,128)(2,1)}, ...), condition=%wide.region_21.21_spmd, body=%wide.region_20.20_spmd.sunk | while | flops 776503296 | bytes 12768005 | solution.py:45
  531.7 1.7 convert_bitcast_fusion.16
  533.5 7.2 %fusion.333 = bf16[18,4,128,128]{2,0,1,3:T(8,128)(2,1)S(1)} fusion(bf16[18,4,128,128,1]{2,3,0,1,4:T(8,128)(2,1)S(1)} %convert_bitcast_fusion.16, bf16[18,18,4,4]{0,1,3,2:T(8,128)(2,1)S(1)} %copy-done.20), kind=kOutput, calls=%fused_computation.133.clone.1 | convolution fusion | flops 171048960 | bytes 4728960 | tf_op jit(solution)/shard_map/cond/branch_1_fun/while/body/eval_jaxpr/wvts,wsac->vtac/dot_general | solution.py:38
  540.7 1.7 fusion.334
  542.4 1.7 convert_bitcast_fusion.16
  544.2 7.2 %fusion.333 = bf16[18,4,128,128]{2,0,1,3:T(8,128)(2,1)S(1)} fusion(bf16[18,4,128,128,1]{2,3,0,1,4:T(8,128)(2,1)S(1)} %convert_bitcast_fusion.16, bf16[18,18,4,4]{0,1,3,2:T(8,128)(2,1)S(1)} %copy-done.20), kind=kOutput, calls=%fused_computation.133.clone.1 | convolution fusion | flops 171048960 | bytes 4728960 | tf_op jit(solution)/shard_map/cond/branch_1_fun/while/body/eval_jaxpr/wvts,wsac->vtac/dot_general | solution.py:38
  551.4 1.7 fusion.334
  553.4 21.3 %while.110 = (s32[]{:T(128)}, bf16[2,18,128,128]{2,3,1,0:T(8,128)(2,1)S(1)}, bf16[2,4,128,128]{2,3,1,0:T(8,128)(2,1)}, bf16[2,18,128,128]{2,3,1,0:T(8,128)(2,1)S...) while((s32[]{:T(128)}, bf16[2,18,128,128]{2,3,1,0:T(8,128)(2,1)S(1)}, ...), condition=%wide.region_23.23_spmd, body=%wide.region_22.22_spmd.sunk | while | flops 776503296 | bytes 12726505 | solution.py:45
  553.4 1.7 convert_bitcast_fusion.17
  555.1 7.2 %fusion.341 = bf16[18,4,128,128]{2,0,1,3:T(8,128)(2,1)S(1)} fusion(bf16[18,4,128,128,1]{2,3,0,1,4:T(8,128)(2,1)S(1)} %convert_bitcast_fusion.17, bf16[18,18,4,4]{0,1,3,2:T(8,128)(2,1)S(1)} %get-tuple-element.1153), kind=kOutput, calls=%fused_computation.153.clone.1 | convolution fusion | flops 171048960 | bytes 4728960 | tf_op jit(solution)/shard_map/cond/branch_1_fun/while/body/eval_jaxpr/wvts,wsac->vtac/dot_general | solution.py:38
  562.3 1.7 fusion.342
  564.1 1.7 convert_bitcast_fusion.17
  565.8 7.2 %fusion.341 = bf16[18,4,128,128]{2,0,1,3:T(8,128)(2,1)S(1)} fusion(bf16[18,4,128,128,1]{2,3,0,1,4:T(8,128)(2,1)S(1)} %convert_bitcast_fusion.17, bf16[18,18,4,4]{0,1,3,2:T(8,128)(2,1)S(1)} %get-tuple-element.1153), kind=kOutput, calls=%fused_computation.153.clone.1 | convolution fusion | flops 171048960 | bytes 4728960 | tf_op jit(solution)/shard_map/cond/branch_1_fun/while/body/eval_jaxpr/wvts,wsac->vtac/dot_general | solution.py:38
  573.0 1.7 fusion.342
  574.7 1.4 copy.177
  576.4 62.9 %psum.39 = f32[]{:T(128)} all-reduce(f32[]{:T(128)} %multiply_reduce_fusion), channel_id=1, replica_groups=mesh['site'=4,'blk'=16,'charge'=2] {'blk','charge'}, use_global_device_ids=true, to_apply=%region_35.36 | all-reduce | flops 1 | bytes 8 | tf_op jit(solution)/shard_map/psum | solution.py:147
  640.0 3.3 fusion.240
  (258 shorter events, 156.4 us)
Async XLA Ops:
  7.2 4.4 copy-start.18
  7.2 5.4 copy-start.17
  7.2 117.0 %all-gather.3.cloned.1.call-start = ((), (), s32[]{:S(2)}) async-start(), calls=%async_computation | async-start | bytes 17825792 | tf_op jit(solution)/shard_map/all_gather | solution.py:124
  8.6 0.5 copy-start.21
  9.1 4.5 copy-start.2
  13.6 2.3 copy-start.26
  13.6 3.4 copy-start.28
  13.6 18.4 %copy-start.25 = (s32[2]{0:T(128)S(1)}, s32[2]{0:T(128)}, u32[]{:S(2)}) copy-start(s32[2]{0:T(128)} %constant.168.clone) | copy-start | bytes 28
  14.7 29.0 %collective-permute-start = (bf16[2,18,128,128]{3,2,1,0:T(8,128)(2,1)}, bf16[2,18,128,128]{3,2,1,0:T(8,128)(2,1)S(1)}, u32[]{:S(2)}, u32[]{:S(2)}) collective-permute-start(bf16[2,18,128,128]{3,2,1,0:T(8,128)(2,1)} %get-tuple-element.585), channel_id=1, source_target_pairs={{0,32},{32,64},{64,96},{1,33},{33,65},{65,97},{2,34},{34,66},{66,9... | collective-permute-start | bytes 3538952 | tf_op jit(solution)/shard_map/ppermute | solution.py:24
  16.0 16.0 %collective-permute-start.3 = (s32[2]{0:T(128)S(1)}, s32[2]{0:T(128)S(1)}, u32[]{:S(2)}, u32[]{:S(2)}) collective-permute-start(s32[2]{0:T(128)S(1)} %bitcast.620), channel_id=1, source_target_pairs={{0,1},{1,0},{2,3},{3,2},{4,5},{5,4},{6,7},{7,6},{8,9},{9,8},{10,11... | collective-permute-start | bytes 32 | tf_op jit(solution)/shard_map/ppermute | solution.py:28
  43.7 1.8 copy-start.8
  45.6 105.5 %collective-permute-start.1 = (bf16[2,18,128,128]{3,2,1,0:T(8,128)(2,1)S(1)}, bf16[2,18,128,128]{3,2,1,0:T(8,128)(2,1)}, u32[]{:S(2)}, u32[]{:S(2)}) collective-permute-start(bf16[2,18,128,128]{3,2,1,0:T(8,128)(2,1)S(1)} %get-tuple-element.587), channel_id=1, source_target_pairs={{0,32},{32,64},{64,96},{1,33},{33,65},{65,97},{2,34},{34,66},{66,9... | collective-permute-start | bytes 3538952 | tf_op jit(solution)/shard_map/ppermute | solution.py:24
  150.3 102.8 %collective-permute-start.4 = (bf16[2,2,128,2048]{3,1,2,0:T(2,128)(2,1)}, bf16[2,2,128,2048]{3,1,2,0:T(2,128)(2,1)}, u32[]{:S(2)}, u32[]{:S(2)}) collective-permute-start(bf16[2,2,128,2048]{3,1,2,0:T(2,128)(2,1)} %fusion.233), channel_id=1, source_target_pairs={{0,1},{1,0},{2,3},{3,2},{4,5},{5,4},{6,7},{7,6},{8,9},{9,8},{10,11... | collective-permute-start | bytes 6291464 | tf_op jit(solution)/shard_map/ppermute | solution.py:28
  151.2 11.4 %copy-start = (bf16[1,2,128,2048]{3,2,1,0:T(8,128)(2,1)S(1)}, bf16[1,2,128,2048]{3,2,1,0:T(8,128)(2,1)}, u32[]{:S(2)}) copy-start(bf16[1,2,128,2048]{3,2,1,0:T(8,128)(2,1)} %param.39) | copy-start | bytes 3145732
  151.2 11.4 %copy-start.22 = (bf16[2,128]{1,0:T(2,128)(2,1)S(1)}, bf16[2,128]{1,0:T(2,128)(2,1)}, u32[]{:S(2)}) copy-start(bf16[2,128]{1,0:T(2,128)(2,1)} %copy-done.21) | copy-start | bytes 1540
  151.6 98.8 %collective-permute-start.2 = (bf16[2,18,128,128]{3,2,1,0:T(8,128)(2,1)S(1)}, bf16[2,18,128,128]{3,2,1,0:T(8,128)(2,1)}, u32[]{:S(2)}, u32[]{:S(2)}) collective-permute-start(bf16[2,18,128,128]{3,2,1,0:T(8,128)(2,1)S(1)} %get-tuple-element.589), channel_id=1, source_target_pairs={{0,32},{32,64},{64,96},{1,33},{33,65},{65,97},{2,34},{34,66},{66,9... | collective-permute-start | bytes 3538952 | tf_op jit(solution)/shard_map/ppermute | solution.py:24
  162.5 87.9 %copy-start.9 = (bf16[2,18,128,128]{3,2,1,0:T(8,128)(2,1)S(1)}, bf16[2,18,128,128]{3,2,1,0:T(8,128)(2,1)}, u32[]{:S(2)}) copy-start(bf16[2,18,128,128]{3,2,1,0:T(8,128)(2,1)} %copy-done.8) | copy-start | bytes 3538948
  265.8 3.9 copy-start.27
  269.7 199.8 %copy-start.23 = (f32[2,128]{1,0:T(2,128)S(1)}, f32[2,128]{1,0:T(2,128)}, u32[]{:S(2)}) copy-start(f32[2,128]{1,0:T(2,128)} %get-tuple-element.729) | copy-start | bytes 3076
  269.7 199.8 %copy-start.24 = (f32[1,2]{1,0:T(1,128)S(1)}, f32[1,2]{1,0:T(1,128)}, u32[]{:S(2)}) copy-start(f32[1,2]{1,0:T(1,128)} %param.45) | copy-start | bytes 28
  269.7 5.2 copy-start.4
  368.0 1.6 copy-start.5
  369.6 5.1 copy-start.4
  467.8 1.6 copy-start.5
  469.5 55.0 %copy-start.1 = (bf16[1,2,128,2048]{3,2,1,0:T(8,128)(2,1)S(1)}, bf16[1,2,128,2048]{3,2,1,0:T(8,128)(2,1)}, u32[]{:S(2)}) copy-start(bf16[1,2,128,2048]{3,2,1,0:T(8,128)(2,1)} %param.39) | copy-start | bytes 3145732
  469.5 55.0 %copy-start.3 = (bf16[2,18,128,128]{3,2,1,0:T(8,128)(2,1)S(1)}, bf16[2,18,128,128]{3,2,1,0:T(8,128)(2,1)}, u32[]{:S(2)}) copy-start(bf16[2,18,128,128]{3,2,1,0:T(8,128)(2,1)} %get-tuple-element.728) | copy-start | bytes 3538948
  531.7 1.7 copy-start.20
  533.4 7.2 %copy-start.14 = (bf16[2,4,128,128]{2,3,1,0:T(8,128)(2,1)S(1)}, bf16[2,4,128,128]{2,3,1,0:T(8,128)(2,1)}, u32[]{:S(2)}) copy-start(bf16[2,4,128,128]{2,3,1,0:T(8,128)(2,1)} %get-tuple-element.1133) | copy-start | bytes 786436 | tf_op jit(solution)/shard_map/cond/branch_1_fun/while
  542.4 1.7 copy-start.20
  544.2 7.2 %copy-start.14 = (bf16[2,4,128,128]{2,3,1,0:T(8,128)(2,1)S(1)}, bf16[2,4,128,128]{2,3,1,0:T(8,128)(2,1)}, u32[]{:S(2)}) copy-start(bf16[2,4,128,128]{2,3,1,0:T(8,128)(2,1)} %get-tuple-element.1133) | copy-start | bytes 786436 | tf_op jit(solution)/shard_map/cond/branch_1_fun/while
  555.1 7.2 %copy-start.11 = (bf16[2,4,128,128]{2,3,1,0:T(8,128)(2,1)S(1)}, bf16[2,4,128,128]{2,3,1,0:T(8,128)(2,1)}, u32[]{:S(2)}) copy-start(bf16[2,4,128,128]{2,3,1,0:T(8,128)(2,1)} %get-tuple-element.1151) | copy-start | bytes 786436 | tf_op jit(solution)/shard_map/cond/branch_1_fun/while
  565.8 7.2 %copy-start.11 = (bf16[2,4,128,128]{2,3,1,0:T(8,128)(2,1)S(1)}, bf16[2,4,128,128]{2,3,1,0:T(8,128)(2,1)}, u32[]{:S(2)}) copy-start(bf16[2,4,128,128]{2,3,1,0:T(8,128)(2,1)} %get-tuple-element.1151) | copy-start | bytes 786436 | tf_op jit(solution)/shard_map/cond/branch_1_fun/while
Sparse Core Ops, SparseCore 0:
  11.7 112.4 all-gather.2
